TPU v7x, 128 devices: a whole 4x4x4 slice. The times are simulated.
128 devices in a mesh: bx: 16 (over x, z), by: 8 (over y, core).
Axes of the slice: x: 4, y: 4, z: 4, core: 2. Of those that a mesh axis runs over, the one named last changes fastest.
Arguments:
- features: bfloat16 [16, 8, 1024, 128], P('bx', 'by'), may hold values from -13 to 13
- live_count: int32 [16, 8], P('bx', 'by'), may hold values from 128 to 1024, as said below
- neighbour_map: int32 [16, 8, 27, 1024], P('bx', 'by'), may hold values from 0 to 2175, as said below
- send_rows: int32 [16, 8, 8, 128], P('bx', 'by'), may hold values from 0 to 1023, as said below
- weight: bfloat16 [3456, 128], replicated, may hold values from -0.109375 to 0.109375
- gain: float32 [128], replicated, may hold values from 0.5 to 1.5
- shift: float32 [128], replicated, may hold values from -3 to 3
- cotangent: bfloat16 [16, 8, 1024, 128], P('bx', 'by'), may hold values from -13 to 13
Outputs:
- activated: bfloat16 [16, 8, 1024, 128], P('bx', 'by')
- grad_features: bfloat16 [16, 8, 1024, 128], P('bx', 'by')
- grad_weight: float32 [27, 128, 128], P(None, 'bx', 'by')
Inputs may be any that keep to these rules, and one draw needn't show every extreme that they name: Rows 0 to live_count - 1 of a brick are live, the rest padding; in every draw some brick is full. `send_rows`: every entry is below its brick's live count; the eight blocks follow the directions (dx, dy) in row-major order with the brick's own position left out. `neighbour_map`: entries index the brick's extended table; offset 13 of a live row names that row itself; every entry of a padding row is 1536. With B = min(1024, 512) and q = r // B for a live row r, an entry below 1024 lies in rows q B to q B + B - 1, and an entry 1024 + b * 128 + h of incoming block b other than 4 has h in q * 128 B / 1024 to (q + 1) * 128 B / 1024 - 1.
All inputs are finite; a program needn't handle non-finite values.
Results may differ from a plain program's by a relative error of at most 0.029.
The roundings to bfloat16 on the way count: a program that leaves them out, or rounds other values in their place, can miss the bound.
Values may be sent and summed in bfloat16 or wider, within the bound.
No kernel may reach another device: no remote copies, remote signals or barrier semaphores. Data moves between devices by JAX's collectives and lax.ppermute only.
A program may use at most 64 MiB of HBM per device.

v0:
```python
import jax
import jax.numpy as jnp
from jax import lax
from jax.sharding import PartitionSpec as P

epsilon = 1e-05


def extended(cells, sides, width):
    for axis, dim in sides:
        count = lax.axis_size(axis)
        ends = count - 1
        head = lax.slice_in_dim(cells, 0, width, axis=dim)
        tail = lax.slice_in_dim(cells, cells.shape[dim] - width, cells.shape[dim], axis=dim)
        cells = jnp.concatenate(
            [
                lax.ppermute(tail, axis, [(i, (i + 1) % count) for i in range(ends)]),
                cells,
                lax.ppermute(head, axis, [((i + 1) % count, i) for i in range(ends)]),
            ],
            axis=dim,
        )
    return cells


def from_neighbours(outgoing):
    padded = extended(outgoing, (("bx", 0), ("by", 1)), 1)
    return padded[::2, ::2]


def per_device(features, live_count, neighbour_map, send_rows, weight, gain, shift, cotangent):
    own_rows = features[0, 0]
    rows_total, channels = own_rows.shape
    halo_rows = send_rows.shape[3]
    block_rows = min(rows_total, 512)
    blocks_count = rows_total // block_rows
    halo_window = halo_rows // blocks_count
    window_rows = block_rows + 9 * halo_window
    sent_index = send_rows[0, 0].reshape(-1)
    send_select = (
        sent_index[:, None] == lax.broadcasted_iota(jnp.int32, (1, rows_total), 1)
    ).astype(jnp.bfloat16)
    chosen_rows = jnp.dot(send_select, own_rows, preferred_element_type=jnp.float32).astype(
        jnp.bfloat16
    )
    chosen_rows = chosen_rows.reshape(8, halo_rows, channels)
    blank_block = jnp.zeros((1, halo_rows, channels), jnp.bfloat16)
    outgoing = jnp.concatenate([chosen_rows[:4], blank_block, chosen_rows[4:]], axis=0).reshape(
        3, 3, halo_rows, channels
    )
    incoming = from_neighbours(outgoing).reshape(9, blocks_count, halo_window, channels)
    index_blocks = neighbour_map[0, 0].reshape(27, blocks_count, block_rows).transpose(1, 0, 2)
    own_blocks = own_rows.reshape(blocks_count, block_rows, channels)
    halo_blocks = incoming.transpose(1, 0, 2, 3)
    block_ids = jnp.arange(blocks_count, dtype=jnp.int32)

    def selector_of(indices, block_index):
        beyond = indices - rows_total
        target = beyond // halo_rows
        inside = beyond - target * halo_rows - block_index * halo_window
        local_pos = indices - block_index * block_rows
        remote_pos = block_rows + target * halo_window + inside
        usable = (inside >= 0) & (inside < halo_window)
        position = jnp.where(indices < rows_total, local_pos, jnp.where(usable, remote_pos, -1))
        return position[:, :, None] == lax.broadcasted_iota(jnp.int32, (1, 1, window_rows), 2)

    def forward_block(pieces):
        indices, own_part, halo_part, block_index = pieces
        window = jnp.concatenate([own_part, halo_part.reshape(9 * halo_window, channels)], axis=0)
        selector = selector_of(indices, block_index).astype(jnp.bfloat16)
        gathered = jnp.einsum(
            "kbw,wc->bkc", selector, window, preferred_element_type=jnp.float32
        ).astype(jnp.bfloat16)
        columns = gathered.reshape(block_rows, 27 * channels)
        return (jnp.dot(columns, weight, preferred_element_type=jnp.float32), columns)

    conv_blocks, column_blocks = lax.map(
        forward_block, (index_blocks, own_blocks, halo_blocks, block_ids)
    )
    conv_out = conv_blocks.reshape(rows_total, channels).astype(jnp.bfloat16)
    conv_float = conv_out.astype(jnp.float32)
    live_mask = (lax.broadcasted_iota(jnp.int32, (rows_total, 1), 0) < live_count[0, 0]).astype(
        jnp.float32
    )
    local_count = jnp.sum(live_mask)
    total_sum, total_count = lax.psum(
        (jnp.sum(conv_float * live_mask, axis=0), local_count), ("bx", "by")
    )
    center = total_sum / total_count
    deviation = (conv_float - center) * live_mask
    variance = lax.psum(jnp.sum(deviation * deviation, axis=0), ("bx", "by")) / total_count
    inverse_std = lax.rsqrt(variance + epsilon)
    normalized = (conv_float - center) * inverse_std
    before = gain * normalized + shift
    activated = (jnp.maximum(before, 0.0) * live_mask).astype(jnp.bfloat16)
    upstream = cotangent[0, 0].astype(jnp.float32) * (before > 0.0) * live_mask
    sum_up, sum_cross = lax.psum(
        (jnp.sum(upstream, axis=0), jnp.sum(upstream * normalized, axis=0)), ("bx", "by")
    )
    conv_grad = (
        gain
        * inverse_std
        * (upstream - live_mask * (sum_up + normalized * sum_cross) / total_count)
    ).astype(jnp.bfloat16)
    grad_blocks = conv_grad.reshape(blocks_count, block_rows, channels)

    def backward_block(weight_acc, pieces):
        indices, columns, grad_rows, block_index = pieces
        weight_acc = weight_acc + lax.dot_general(
            columns, grad_rows, (((0,), (0,)), ((), ())), preferred_element_type=jnp.float32
        )
        column_grad = lax.dot_general(
            grad_rows, weight, (((1,), (1,)), ((), ())), preferred_element_type=jnp.float32
        )
        column_grad = column_grad.reshape(block_rows, 27, channels)
        selector = selector_of(indices, block_index).astype(jnp.float32)
        window_grad = jnp.einsum(
            "kbw,bkc->wc",
            selector,
            column_grad,
            precision=lax.Precision.HIGHEST,
            preferred_element_type=jnp.float32,
        )
        return (
            weight_acc,
            (window_grad[:block_rows], window_grad[block_rows:].reshape(9, halo_window, channels)),
        )

    start_acc = jnp.zeros((27 * channels, channels), jnp.float32)
    weight_acc, (own_parts, halo_parts) = lax.scan(
        backward_block, start_acc, (index_blocks, column_blocks, grad_blocks, block_ids)
    )
    weight_terms = weight_acc.reshape(27, channels, channels)
    partial_x = lax.psum_scatter(
        weight_terms.astype(jnp.bfloat16), "bx", scatter_dimension=1, tiled=True
    )
    summed = lax.psum_scatter(partial_x, "by", scatter_dimension=2, tiled=True).astype(jnp.float32)
    grad_weight = summed / jnp.sqrt(total_count)
    own_table = own_parts.reshape(rows_total, channels)
    halo_table = halo_parts.transpose(1, 0, 2, 3).reshape(3, 3, halo_rows, channels)
    halo_grad = halo_table.astype(jnp.bfloat16)
    returned = from_neighbours(halo_grad).reshape(9, halo_rows, channels)
    slots_back = (
        jnp.concatenate([returned[:4], returned[5:]], axis=0)
        .reshape(-1, channels)
        .astype(jnp.float32)
    )
    added_back = lax.dot_general(
        send_select.astype(jnp.float32),
        slots_back,
        (((0,), (0,)), ((), ())),
        precision=lax.Precision.HIGHEST,
        preferred_element_type=jnp.float32,
    )
    own_grad = own_table + added_back
    return (activated[None, None], own_grad.astype(jnp.bfloat16)[None, None], grad_weight)


def solution(mesh):
    return jax.shard_map(
        per_device,
        mesh=mesh,
        in_specs=(
            P("bx", "by", None, None),
            P("bx", "by"),
            P("bx", "by", None, None),
            P("bx", "by", None, None),
            P(),
            P(),
            P(),
            P("bx", "by", None, None),
        ),
        out_specs=(P("bx", "by", None, None), P("bx", "by", None, None), P(None, "bx", "by")),
        check_vma=False,
    )
```

profile of v0, /device:TPU:1, one launch (start us, length us, event | category | flops | bytes accessed | tf_op | source)
XLA Modules:
  0.0 463.2 jit_solution(409183118276341036)
XLA Ops:
  7.2 1.9 fusion.34
  9.1 4.4 collective-permute-start
  13.5 1.3 collective-permute-start.1
  15.7 3.4 collective-permute-done.1
  19.0 0.8 pad_maximum_fusion.9
  19.8 5.0 %collective-permute-start.2 = (bf16[5,1,128,128]{3,2,1,0:T(8,128)(2,1)}, bf16[5,1,128,128]{3,2,1,0:T(8,128)(2,1)}, u32[]{:S(2)}, u32[]{:S(2)}) collective-permute-start(bf16[5,1,128,128]{3,2,1,0:T(8,128)(2,1)} %get-tuple-element.372), channel_id=1, source_target_pairs={{0,1},{1,2},{2,3},{3,4},{4,5},{5,6},{6,7},{8,9},{9,10},{10,11},{11... | collective-permute-start | bytes 491528 | tf_op jit(solution)/shard_map/ppermute | solution.py:17
  24.8 1.9 collective-permute-start.3
  26.8 1.2 reduce.4
  28.7 3.0 collective-permute-done.3
  31.8 1.1 pad_maximum_fusion
  33.0 38.2 %while.33 = (s32[]{:T(128)}, bf16[2,512,128]{2,1,0:T(8,128)(2,1)S(1)}, bf16[2,512,3456]{1,2,0:T(8,128)(2,1)}, bf16[2,512,128]{2,1,0:T(8,128)(2,1)}, bf16[2,9,64,...) while((s32[]{:T(128)}, ...), condition=%wide.region_1.2_spmd.clone, body=%wide.region_0.1_spmd.sunk.clone | while | flops 4321123840 | bytes 16304801 | solution.py:77
  35.0 0.9 dynamic-slice_bitcast_fusion.3
  35.9 13.0 %fusion.82 = bf16[128,27,512]{2,0,1:T(8,128)(2,1)S(1)} fusion(s32[27,512]{1,0:T(8,128)S(1)} %bitcast_select_fusion.6, bf16[576,128]{1,0:T(8,128)(2,1)S(1)} %bitcast.223, bf16[512,128]{1,0:T(8,128)(2,1)S(1)} %dynamic-slice_bitcast_fusion.3), kind=kOutput, calls=%fused_computation.3.clone.1.clone | convolution fusion | flops 3867738112 | bytes 3872768 | tf_op jit(solution)/shard_map/while/body/eval_jaxpr/kbw,wc->bkc/dot_general | solution.py:71
  48.9 2.0 constant_dynamic-update-slice_fusion.6
  50.8 1.2 fusion.83
  54.0 0.9 dynamic-slice_bitcast_fusion.3
  55.0 13.0 %fusion.82 = bf16[128,27,512]{2,0,1:T(8,128)(2,1)S(1)} fusion(s32[27,512]{1,0:T(8,128)S(1)} %bitcast_select_fusion.6, bf16[576,128]{1,0:T(8,128)(2,1)S(1)} %bitcast.223, bf16[512,128]{1,0:T(8,128)(2,1)S(1)} %dynamic-slice_bitcast_fusion.3), kind=kOutput, calls=%fused_computation.3.clone.1.clone | convolution fusion | flops 3867738112 | bytes 3872768 | tf_op jit(solution)/shard_map/while/body/eval_jaxpr/kbw,wc->bkc/dot_general | solution.py:71
  67.9 2.0 constant_dynamic-update-slice_fusion.6
  70.0 1.2 fusion.83
  71.4 66.2 %all-reduce.2 = (f32[128]{0:T(128)S(1)}, f32[]{:T(128)}) all-reduce(f32[128]{0:T(128)S(1)} %multiply_reduce_fusion.1, f32[]{:T(128)} %fusion.44), channel_id=1, replica_groups=mesh['bx'=16,'by'=8] {'bx','by'}, use_global_device_ids=true, to_apply=%region_3.4 | all-reduce | flops 129 | bytes 1032 | tf_op jit(solution)/shard_map/psum | solution.py:86
  138.4 62.9 %psum.37 = f32[128]{0:T(128)S(1)} all-reduce(f32[128]{0:T(128)S(1)} %multiply_reduce_fusion), channel_id=1, replica_groups=mesh['bx'=16,'by'=8] {'bx','by'}, use_global_device_ids=true, to_apply=%region_7.8 | all-reduce | flops 128 | bytes 1024 | tf_op jit(solution)/shard_map/psum | solution.py:91
  202.0 1.2 fusion.39
  203.1 64.0 %all-reduce.1 = (f32[128]{0:T(128)S(1)}, f32[128]{0:T(128)S(1)}) all-reduce(f32[128]{0:T(128)S(1)} %get-tuple-element.329, f32[128]{0:T(128)S(1)} %get-tuple-element.328), channel_id=1, replica_groups=mesh['bx'=16,'by'=8] {'bx','by'}, use_global_device_ids=true, to_apply=%region_11.12 | all-reduce | flops 256 | bytes 2048 | tf_op jit(solution)/shard_map/psum | solution.py:97
  267.1 1.9 fusion.42
  269.0 73.1 %while.34 = (s32[]{:T(128)}, f32[3456,128]{1,0:T(8,128)S(1)}, f32[2,512,128]{2,1,0:T(8,128)}, bf16[2,9,64,128]{3,2,0,1:T(8,128)(2,1)}, bf16[2,512,3456]{1,2,0:T(...) while((s32[]{:T(128)}, f32[3456,128]{1,0:T(8,128)S(1)}, ...), condition=%wide.region_13.14_spmd.clone.clone, body=%wide.region_12.13_spmd.clone.sunk.clone | while | flops 24024522752 | bytes 28413672 | solution.py:130
  271.0 1.1 fusion.89
  272.1 28.7 %fusion.90 = f32[1088,128]{1,0:T(8,128)S(1)} fusion(f32[512,27,128]{2,0,1:T(8,128)S(1)} %fusion.89, s32[27,512]{1,0:T(8,128)S(1)} %bitcast_select_fusion.7), kind=kOutput, calls=%fused_computation.31.clone.1.clone | convolution fusion | flops 23117266944 | bytes 7690240 | tf_op jit(solution)/shard_map/while/body/eval_jaxpr/kbw,bkc->wc/dot_general | solution.py:117
  302.4 3.2 convolution_add_fusion.3
  307.6 1.1 fusion.89
  308.7 28.7 %fusion.90 = f32[1088,128]{1,0:T(8,128)S(1)} fusion(f32[512,27,128]{2,0,1:T(8,128)S(1)} %fusion.89, s32[27,512]{1,0:T(8,128)S(1)} %bitcast_select_fusion.7), kind=kOutput, calls=%fused_computation.31.clone.1.clone | convolution fusion | flops 23117266944 | bytes 7690240 | tf_op jit(solution)/shard_map/while/body/eval_jaxpr/kbw,bkc->wc/dot_general | solution.py:117
  338.9 3.2 convolution_add_fusion.3
  342.2 1.0 convert_element_type.131
  343.3 1.0 fusion.48
  344.3 1.3 collective-permute-start.4
  345.6 1.3 collective-permute-start.5
  348.8 4.0 collective-permute-done.5
  352.8 1.0 pad_maximum_fusion.6
  353.8 3.6 collective-permute-start.6
  357.4 1.9 collective-permute-start.7
  359.4 0.9 multiply_convert_fusion
  360.3 3.8 collective-permute-done.7
  364.1 1.1 pad_maximum_fusion.1
  365.2 59.0 %all-reduce.5.cloned.1.call-done = bf16[27,128,128]{2,1,0:T(8,128)(2,1)} async-done(((bf16[27,128,128]{2,1,0:T(8,128)(2,1)}), bf16[27,128,128]{2,1,0:T(8,128)(2,1)}) %all-reduce.5.cloned.1.call-update) | async-done | bytes 884752
  424.3 0.8 constant_dynamic-slice_fusion.1
  425.1 0.9 copy.30
  426.0 3.2 fusion.35
  429.2 25.7 %reduce-scatter.3.cloned.1.call-done = bf16[27,8,16]{0,1,2:T(8,128)(2,1)} async-done(((bf16[27,8,128]{0,1,2:T(8,128)(2,1)}), bf16[27,8,16]{0,1,2:T(8,128)(2,1)}) %reduce-scatter.3.cloned.1.call-update) | async-done | bytes 6928 | tf_op jit(solution)/shard_map/reduce_scatter | solution.py:137
  454.9 0.8 convert_divide_fusion
  (68 shorter events, 9.8 us)
Async XLA Ops:
  7.2 25.8 %copy-start = (bf16[3456,128]{1,0:T(8,128)(2,1)S(1)}, bf16[3456,128]{1,0:T(8,128)(2,1)}, u32[]{:S(2)}) copy-start(bf16[3456,128]{1,0:T(8,128)(2,1)} %param.16) | copy-start | bytes 2654212
  7.2 417.1 %all-reduce.5.cloned.1.call-start = ((), (), s32[]{:S(2)}) async-start(), calls=%async_computation.2 | async-start | bytes 1769472
  9.1 6.5 %collective-permute-start = (bf16[1,3,128,128]{3,2,1,0:T(8,128)(2,1)S(1)}, bf16[1,3,128,128]{3,2,1,0:T(8,128)(2,1)S(1)}, u32[]{:S(2)}, u32[]{:S(2)}) collective-permute-start(bf16[1,3,128,128]{3,2,1,0:T(8,128)(2,1)S(1)} %bitcast.239), channel_id=1, source_target_pairs={{0,8},{8,16},{16,24},{24,32},{32,40},{40,48},{48,56},{56,64},{64,7... | collective-permute-start | bytes 294920 | tf_op jit(solution)/shard_map/ppermute | solution.py:17
  13.5 5.5 %collective-permute-start.1 = (bf16[1,3,128,128]{3,2,1,0:T(8,128)(2,1)S(1)}, bf16[1,3,128,128]{3,2,1,0:T(8,128)(2,1)S(1)}, u32[]{:S(2)}, u32[]{:S(2)}) collective-permute-start(bf16[1,3,128,128]{3,2,1,0:T(8,128)(2,1)S(1)} %bitcast.238), channel_id=1, source_target_pairs={{8,0},{16,8},{24,16},{32,24},{40,32},{48,40},{56,48},{64,56},{72,6... | collective-permute-start | bytes 294920 | tf_op jit(solution)/shard_map/ppermute | solution.py:19
  19.8 8.9 %collective-permute-start.2 = (bf16[5,1,128,128]{3,2,1,0:T(8,128)(2,1)}, bf16[5,1,128,128]{3,2,1,0:T(8,128)(2,1)}, u32[]{:S(2)}, u32[]{:S(2)}) collective-permute-start(bf16[5,1,128,128]{3,2,1,0:T(8,128)(2,1)} %get-tuple-element.372), channel_id=1, source_target_pairs={{0,1},{1,2},{2,3},{3,4},{4,5},{5,6},{6,7},{8,9},{9,10},{10,11},{11... | collective-permute-start | bytes 491528 | tf_op jit(solution)/shard_map/ppermute | solution.py:17
  24.8 7.0 %collective-permute-start.3 = (bf16[5,1,128,128]{3,2,1,0:T(8,128)(2,1)}, bf16[5,1,128,128]{3,2,1,0:T(8,128)(2,1)}, u32[]{:S(2)}, u32[]{:S(2)}) collective-permute-start(bf16[5,1,128,128]{3,2,1,0:T(8,128)(2,1)} %get-tuple-element.373), channel_id=1, source_target_pairs={{1,0},{2,1},{3,2},{4,3},{5,4},{6,5},{7,6},{9,8},{10,9},{11,10},{12... | collective-permute-start | bytes 491528 | tf_op jit(solution)/shard_map/ppermute | solution.py:19
  32.9 168.4 %copy-start.1 = (f32[128]{0:T(128)S(1)}, f32[128]{0:T(128)}, u32[]{:S(2)}) copy-start(f32[128]{0:T(128)} %param.17) | copy-start | bytes 1540
  32.9 169.0 %copy-start.2 = (f32[128]{0:T(128)S(1)}, f32[128]{0:T(128)}, u32[]{:S(2)}) copy-start(f32[128]{0:T(128)} %param.18) | copy-start | bytes 1540
  269.0 77.9 %copy-start.6 = (u32[128]{0:T(128)S(1)}, u32[128]{0:T(128)}, u32[]{:S(2)}) copy-start(u32[128]{0:T(128)} %constant.182) | copy-start | bytes 1540
  272.1 28.7 %copy-start.3 = (f32[2,512,128]{2,1,0:T(8,128)S(1)}, f32[2,512,128]{2,1,0:T(8,128)}, u32[]{:S(2)}) copy-start(f32[2,512,128]{2,1,0:T(8,128)} %get-tuple-element.580) | copy-start | bytes 1572868 | tf_op jit(solution)/shard_map/while
  300.9 0.8 copy-start.4
  308.7 28.7 %copy-start.3 = (f32[2,512,128]{2,1,0:T(8,128)S(1)}, f32[2,512,128]{2,1,0:T(8,128)}, u32[]{:S(2)}) copy-start(f32[2,512,128]{2,1,0:T(8,128)} %get-tuple-element.580) | copy-start | bytes 1572868 | tf_op jit(solution)/shard_map/while
  337.5 0.8 copy-start.4
  342.2 83.8 %copy-start.5 = (s32[1,1,8,128]{3,2,1,0:T(8,128)S(1)}, s32[1,1,8,128]{3,2,1,0:T(8,128)}, u32[]{:S(2)}) copy-start(s32[1,1,8,128]{3,2,1,0:T(8,128)} %param.15) | copy-start | bytes 12292
  343.2 111.7 %reduce-scatter.3.cloned.1.call-start = ((), (), s32[]{:S(2)}) async-start(), calls=%async_computation.1 | async-start | bytes 294912 | tf_op jit(solution)/shard_map/reduce_scatter | solution.py:137
  344.3 4.6 collective-permute-start.4
  345.6 7.3 %collective-permute-start.5 = (bf16[1,3,128,128]{3,2,1,0:T(8,128)(2,1)S(1)}, bf16[1,3,128,128]{3,2,1,0:T(8,128)(2,1)S(1)}, u32[]{:S(2)}, u32[]{:S(2)}) collective-permute-start(bf16[1,3,128,128]{3,2,1,0:T(8,128)(2,1)S(1)} %bitcast.236), channel_id=1, source_target_pairs={{8,0},{16,8},{24,16},{32,24},{40,32},{48,40},{56,48},{64,56},{72,6... | collective-permute-start | bytes 294920 | tf_op jit(solution)/shard_map/ppermute | solution.py:19
  353.8 6.4 %collective-permute-start.6 = (bf16[5,1,128,128]{3,2,1,0:T(8,128)(2,1)S(1)}, bf16[5,1,128,128]{3,2,1,0:T(8,128)(2,1)S(1)}, u32[]{:S(2)}, u32[]{:S(2)}) collective-permute-start(bf16[5,1,128,128]{3,2,1,0:T(8,128)(2,1)S(1)} %get-tuple-element.370), channel_id=1, source_target_pairs={{0,1},{1,2},{2,3},{3,4},{4,5},{5,6},{6,7},{8,9},{9,10},{10,11},{11... | collective-permute-start | bytes 491528 | tf_op jit(solution)/shard_map/ppermute | solution.py:17
  357.4 6.6 %collective-permute-start.7 = (bf16[5,1,128,128]{3,2,1,0:T(8,128)(2,1)S(1)}, bf16[5,1,128,128]{3,2,1,0:T(8,128)(2,1)S(1)}, u32[]{:S(2)}, u32[]{:S(2)}) collective-permute-start(bf16[5,1,128,128]{3,2,1,0:T(8,128)(2,1)S(1)} %get-tuple-element.371), channel_id=1, source_target_pairs={{1,0},{2,1},{3,2},{4,3},{5,4},{6,5},{7,6},{9,8},{10,9},{11,10},{12... | collective-permute-start | bytes 491528 | tf_op jit(solution)/shard_map/ppermute | solution.py:19
Sparse Core Ops, SparseCore 0:
  343.4 80.8 all-reduce.4
  426.6 28.2 reduce-scatter.2
where the time goes:
time: 466 us; the launch traced here: 463 us
  blocking collectives  193 us (41%)
  matrix products  99.4 us (21%)
  waiting for transfers between devices  99 us (21%)
  starting transfers between devices  20.8 us (4%)
  between operations  16.4 us (4%)
  local copies, waits for them, and re-layouts  15.4 us (3%)
  other arithmetic  13.7 us (3%)
  loops' own time  5.44 us (1%)
    psum x1, blocking collectives, per_device(): lax.psum((jnp.sum(conv_float * live_mask, axis=0), local_count), ('bx', '...  66.2 us
    psum x1, blocking collectives, per_device(): lax.psum((jnp.sum(upstream, axis=0), jnp.sum(upstream * normalized, axis=...  64 us
    psum x1, blocking collectives, per_device(): lax.psum(jnp.sum(deviation * deviation, axis=0), ('bx', 'by')) / total_count  62.9 us
    unnamed x3, waiting for transfers between devices  59.1 us
    dot_general x2, matrix products, backward_block(): jnp.einsum('kbw,bkc->wc', selector, column_grad, precision=lax.Precision....  57.4 us
    dot_general x2, matrix products, forward_block(): jnp.einsum('kbw,wc->bkc', selector, window, preferred_element_type=jnp.fl...  25.9 us
    reduce_scatter x1, waiting for transfers between devices, per_device(): lax.psum_scatter(partial_x, 'by', scatter_dimension=2, tiled=True)  25.7 us
    ppermute x4, starting transfers between devices, extended(): lax.ppermute(tail, axis, [(i, (i + 1) % count) for i in range(ends)])  14.3 us
  transfers between devices with their start and end apart: 10, of which 6 were waited for; matrix products, arithmetic and copies ran while one was open for 2% of the time, Pallas kernels for 0%

commit v1 on v0

--- a/solution.py
+++ b/solution.py
@@ -4,6 +4,7 @@
 from jax.sharding import PartitionSpec as P
 
 epsilon = 1e-05
+axes = ("bx", "by")
 
 
 def extended(cells, sides, width):
@@ -28,6 +29,12 @@
     return padded[::2, ::2]
 
 
+def everyones(rows):
+    devices = lax.axis_size("bx") * lax.axis_size("by")
+    copies = jnp.broadcast_to(rows[None], (devices,) + rows.shape)
+    return lax.all_to_all(copies, axes, 0, 0, tiled=True)
+
+
 def per_device(features, live_count, neighbour_map, send_rows, weight, gain, shift, cotangent):
     own_rows = features[0, 0]
     rows_total, channels = own_rows.shape
@@ -35,7 +42,8 @@
     block_rows = min(rows_total, 512)
     blocks_count = rows_total // block_rows
     halo_window = halo_rows // blocks_count
-    window_rows = block_rows + 9 * halo_window
+    window_rows = block_rows + 8 * halo_window
+    bx, by = lax.axis_size("bx"), lax.axis_size("by")
     sent_index = send_rows[0, 0].reshape(-1)
     send_select = (
         sent_index[:, None] == lax.broadcasted_iota(jnp.int32, (1, rows_total), 1)
@@ -48,7 +56,10 @@
     outgoing = jnp.concatenate([chosen_rows[:4], blank_block, chosen_rows[4:]], axis=0).reshape(
         3, 3, halo_rows, channels
     )
-    incoming = from_neighbours(outgoing).reshape(9, blocks_count, halo_window, channels)
+    incoming = from_neighbours(outgoing).reshape(9, halo_rows, channels)
+    incoming = jnp.concatenate([incoming[:4], incoming[5:]], axis=0).reshape(
+        8, blocks_count, halo_window, channels
+    )
     index_blocks = neighbour_map[0, 0].reshape(27, blocks_count, block_rows).transpose(1, 0, 2)
     own_blocks = own_rows.reshape(blocks_count, block_rows, channels)
     halo_blocks = incoming.transpose(1, 0, 2, 3)
@@ -59,14 +70,15 @@
         target = beyond // halo_rows
         inside = beyond - target * halo_rows - block_index * halo_window
         local_pos = indices - block_index * block_rows
-        remote_pos = block_rows + target * halo_window + inside
-        usable = (inside >= 0) & (inside < halo_window)
+        slot = target - (target > 4)
+        remote_pos = block_rows + slot * halo_window + inside
+        usable = (inside >= 0) & (inside < halo_window) & (target != 4)
         position = jnp.where(indices < rows_total, local_pos, jnp.where(usable, remote_pos, -1))
         return position[:, :, None] == lax.broadcasted_iota(jnp.int32, (1, 1, window_rows), 2)
 
     def forward_block(pieces):
         indices, own_part, halo_part, block_index = pieces
-        window = jnp.concatenate([own_part, halo_part.reshape(9 * halo_window, channels)], axis=0)
+        window = jnp.concatenate([own_part, halo_part.reshape(8 * halo_window, channels)], axis=0)
         selector = selector_of(indices, block_index).astype(jnp.bfloat16)
         gathered = jnp.einsum(
             "kbw,wc->bkc", selector, window, preferred_element_type=jnp.float32
@@ -82,21 +94,27 @@
     live_mask = (lax.broadcasted_iota(jnp.int32, (rows_total, 1), 0) < live_count[0, 0]).astype(
         jnp.float32
     )
-    local_count = jnp.sum(live_mask)
-    total_sum, total_count = lax.psum(
-        (jnp.sum(conv_float * live_mask, axis=0), local_count), ("bx", "by")
-    )
-    center = total_sum / total_count
-    deviation = (conv_float - center) * live_mask
-    variance = lax.psum(jnp.sum(deviation * deviation, axis=0), ("bx", "by")) / total_count
+    local_count = live_count[0, 0].astype(jnp.float32)
+    local_mean = jnp.sum(conv_float * live_mask, axis=0) / local_count
+    local_dev = (conv_float - local_mean) * live_mask
+    local_square = jnp.sum(local_dev * local_dev, axis=0)
+    stats = everyones(
+        jnp.stack([local_mean, local_square, jnp.full((channels,), local_count)])
+    ).reshape(bx * by, 3, channels)
+    counts = stats[:, 2]
+    total_count = jnp.sum(counts, axis=0)
+    center = jnp.sum(stats[:, 0] * counts, axis=0) / total_count
+    apart = stats[:, 0] - center
+    variance = jnp.sum(stats[:, 1] + counts * apart * apart, axis=0) / total_count
     inverse_std = lax.rsqrt(variance + epsilon)
     normalized = (conv_float - center) * inverse_std
     before = gain * normalized + shift
     activated = (jnp.maximum(before, 0.0) * live_mask).astype(jnp.bfloat16)
     upstream = cotangent[0, 0].astype(jnp.float32) * (before > 0.0) * live_mask
-    sum_up, sum_cross = lax.psum(
-        (jnp.sum(upstream, axis=0), jnp.sum(upstream * normalized, axis=0)), ("bx", "by")
-    )
+    sums = everyones(
+        jnp.stack([jnp.sum(upstream, axis=0), jnp.sum(upstream * normalized, axis=0)])
+    ).reshape(bx * by, 2, channels)
+    sum_up, sum_cross = jnp.sum(sums[:, 0], axis=0), jnp.sum(sums[:, 1], axis=0)
     conv_grad = (
         gain
         * inverse_std
@@ -111,45 +129,44 @@
         )
         column_grad = lax.dot_general(
             grad_rows, weight, (((1,), (1,)), ((), ())), preferred_element_type=jnp.float32
-        )
+        ).astype(jnp.bfloat16)
         column_grad = column_grad.reshape(block_rows, 27, channels)
-        selector = selector_of(indices, block_index).astype(jnp.float32)
+        selector = selector_of(indices, block_index).astype(jnp.bfloat16)
         window_grad = jnp.einsum(
             "kbw,bkc->wc",
             selector,
             column_grad,
-            precision=lax.Precision.HIGHEST,
             preferred_element_type=jnp.float32,
         )
         return (
             weight_acc,
-            (window_grad[:block_rows], window_grad[block_rows:].reshape(9, halo_window, channels)),
+            (window_grad[:block_rows], window_grad[block_rows:].reshape(8, halo_window, channels)),
         )
 
     start_acc = jnp.zeros((27 * channels, channels), jnp.float32)
     weight_acc, (own_parts, halo_parts) = lax.scan(
         backward_block, start_acc, (index_blocks, column_blocks, grad_blocks, block_ids)
     )
-    weight_terms = weight_acc.reshape(27, channels, channels)
-    partial_x = lax.psum_scatter(
-        weight_terms.astype(jnp.bfloat16), "bx", scatter_dimension=1, tiled=True
+    weight_terms = weight_acc.astype(jnp.bfloat16).reshape(
+        27, bx, channels // bx, by, channels // by
     )
-    summed = lax.psum_scatter(partial_x, "by", scatter_dimension=2, tiled=True).astype(jnp.float32)
-    grad_weight = summed / jnp.sqrt(total_count)
+    pieces = weight_terms.transpose(1, 3, 0, 2, 4).reshape(bx * by, 27, channels)
+    pieces = jnp.pad(pieces, ((0, 0), (0, 5), (0, 0)))
+    arrived = lax.all_to_all(pieces, axes, 0, 0, tiled=True)
+    summed = jnp.sum(arrived[:, :27].astype(jnp.float32), axis=0)
+    grad_weight = summed.reshape(27, channels // bx, channels // by) / jnp.sqrt(total_count[0])
     own_table = own_parts.reshape(rows_total, channels)
-    halo_table = halo_parts.transpose(1, 0, 2, 3).reshape(3, 3, halo_rows, channels)
+    halo_table = halo_parts.transpose(1, 0, 2, 3).reshape(8, halo_rows, channels)
     halo_grad = halo_table.astype(jnp.bfloat16)
+    halo_grad = jnp.concatenate([halo_grad[:4], blank_block, halo_grad[4:]], axis=0).reshape(
+        3, 3, halo_rows, channels
+    )
     returned = from_neighbours(halo_grad).reshape(9, halo_rows, channels)
-    slots_back = (
-        jnp.concatenate([returned[:4], returned[5:]], axis=0)
-        .reshape(-1, channels)
-        .astype(jnp.float32)
-    )
+    slots_back = jnp.concatenate([returned[:4], returned[5:]], axis=0).reshape(-1, channels)
     added_back = lax.dot_general(
-        send_select.astype(jnp.float32),
+        send_select,
         slots_back,
         (((0,), (0,)), ((), ())),
-        precision=lax.Precision.HIGHEST,
         preferred_element_type=jnp.float32,
     )
     own_grad = own_table + added_back

time: 466 us -> 219 us (0.47)
  blocking collectives: 193 us -> 20.7 us
  waiting for transfers between devices: 99 us -> 32.7 us
  matrix products: 99.4 us -> 68.2 us
  local copies, waits for them, and re-layouts: 15.4 us -> 46.1 us
  between operations: 16.4 us -> 1.86 us
  starting transfers between devices: 20.8 us -> 31.2 us
    psum x3 -> x0, blocking collectives: 193 us -> none  [the longest x1 66.2 us: per_device(): lax.psum((jnp.sum(conv_float * live_mask, axis=0), local_count), ('bx', '...]
    unnamed x3 -> x0, waiting for transfers between devices: 59.1 us -> none
    dot_general x3, matrix products: 60.6 us -> 23.5 us  [the longest x2 21.3 us: backward_block(): jnp.einsum('kbw,bkc->wc', selector, column_grad, preferred_element_type=j...]
    reduce_scatter x1 -> x0, waiting for transfers between devices: 25.7 us -> none  [per_device(): lax.psum_scatter(partial_x, 'by', scatter_dimension=2, tiled=True)]
    all_to_all x0 -> x1, blocking collectives: none -> 20.7 us  [everyones(): return lax.all_to_all(copies, axes, 0, 0, tiled=True)]
    unnamed x13 -> x27, local copies, waits for them, and re-layouts: 2.08 us -> 16.2 us
    all_to_all x0 -> x2, waiting for transfers between devices: none -> 9.83 us  [the longest x1 9.82 us: everyones(): return lax.all_to_all(copies, axes, 0, 0, tiled=True)]
    ppermute x4, waiting for transfers between devices: 0.01 us -> 9.57 us  [extended(): lax.ppermute(tail, axis, [(i, (i + 1) % count) for i in range(ends)])]
where the time goes in v1:
time: 219 us; the launch traced here: 217 us
  matrix products  68.2 us (31%)
  local copies, waits for them, and re-layouts  46.1 us (21%)
  waiting for transfers between devices  32.7 us (15%)
  starting transfers between devices  31.2 us (14%)
  blocking collectives  20.7 us (9%)
  other arithmetic  10.5 us (5%)
  loops' own time  5.52 us (3%)
    dot_general x2, matrix products, forward_block(): jnp.einsum('kbw,wc->bkc', selector, window, preferred_element_type=jnp.fl...  26.7 us
    dot_general x2, matrix products, backward_block(): jnp.einsum('kbw,bkc->wc', selector, column_grad, preferred_element_type=j...  21.3 us
    all_to_all x1, blocking collectives, everyones(): return lax.all_to_all(copies, axes, 0, 0, tiled=True)  20.7 us
    unnamed x27, local copies, waits for them, and re-layouts  16.2 us
    ppermute x4, starting transfers between devices, extended(): lax.ppermute(tail, axis, [(i, (i + 1) % count) for i in range(ends)])  15.8 us
    ppermute x4, waiting for transfers between devices, extended(): lax.ppermute(head, axis, [((i + 1) % count, i) for i in range(ends)])  13.3 us
    all_to_all x1, waiting for transfers between devices, everyones(): return lax.all_to_all(copies, axes, 0, 0, tiled=True)  9.82 us
    ppermute x4, waiting for transfers between devices, extended(): lax.ppermute(tail, axis, [(i, (i + 1) % count) for i in range(ends)])  9.57 us
  transfers between devices with their start and end apart: 10, of which 6 were waited for; matrix products, arithmetic and copies ran while one was open for 2% of the time, Pallas kernels for 0%

profile of v1, /device:TPU:1, one launch (start us, length us, event | category | flops | bytes accessed | tf_op | source)
XLA Modules:
  0.0 216.8 jit_solution(12781356960280811819)
XLA Ops:
  0.6 1.8 fusion.33
  2.5 4.4 %collective-permute-start = (bf16[1,3,128,128]{3,2,1,0:T(8,128)(2,1)S(1)}, bf16[1,3,128,128]{3,2,1,0:T(8,128)(2,1)S(1)}, u32[]{:S(2)}, u32[]{:S(2)}) collective-permute-start(bf16[1,3,128,128]{3,2,1,0:T(8,128)(2,1)S(1)} %bitcast.276), channel_id=1, source_target_pairs={{0,8},{8,16},{16,24},{24,32},{32,40},{40,48},{48,56},{56,64},{64,7... | collective-permute-start | bytes 294920 | tf_op jit(solution)/shard_map/ppermute | solution.py:18
  6.9 1.3 collective-permute-start.1
  9.1 3.4 %collective-permute-done.1 = bf16[1,3,128,128]{3,2,1,0:T(8,128)(2,1)S(1)} collective-permute-done((bf16[1,3,128,128]{3,2,1,0:T(8,128)(2,1)S(1)}, bf16[1,3,128,128]{3,2,1,0:T(8,128)(2,1)S(1)}, u32[]{:S(2)}, u32[]{:S(2)}) %collective-permute-start.1) | collective-permute-done | bytes 98336 | tf_op jit(solution)/shard_map/ppermute | solution.py:20
  12.5 5.0 %collective-permute-start.2 = (bf16[5,1,128,128]{3,2,1,0:T(8,128)(2,1)S(1)}, bf16[5,1,128,128]{3,2,1,0:T(8,128)(2,1)S(1)}, u32[]{:S(2)}, u32[]{:S(2)}) collective-permute-start(bf16[5,1,128,128]{3,2,1,0:T(8,128)(2,1)S(1)} %get-tuple-element.425), channel_id=1, source_target_pairs={{0,1},{1,2},{2,3},{3,4},{4,5},{5,6},{6,7},{8,9},{9,10},{10,11},{11... | collective-permute-start | bytes 491528 | tf_op jit(solution)/shard_map/ppermute | solution.py:18
  17.5 1.9 collective-permute-start.3
  20.6 3.5 %collective-permute-done.3 = bf16[5,1,128,128]{3,2,1,0:T(8,128)(2,1)S(1)} collective-permute-done((bf16[5,1,128,128]{3,2,1,0:T(8,128)(2,1)S(1)}, bf16[5,1,128,128]{3,2,1,0:T(8,128)(2,1)S(1)}, u32[]{:S(2)}, u32[]{:S(2)}) %collective-permute-start.3) | collective-permute-done | bytes 163872 | tf_op jit(solution)/shard_map/ppermute | solution.py:20
  24.4 41.7 %while.33 = (s32[]{:T(128)}, bf16[2,512,128]{2,1,0:T(8,128)(2,1)S(1)}, bf16[2,512,3456]{1,2,0:T(8,128)(2,1)}, bf16[2,512,128]{2,1,0:T(8,128)(2,1)S(1)}, bf16[2,8...) while((s32[]{:T(128)}, ...), condition=%wide.region_1.2_spmd.clone, body=%wide.region_0.1_spmd.sunk.clone | while | flops 4093783040 | bytes 16779936 | solution.py:89
  27.5 13.4 %fusion.85 = bf16[128,27,512]{2,0,1:T(8,128)(2,1)S(1)} fusion(s32[27,512]{1,0:T(8,128)S(1)} %bitcast_select_fusion.6, bf16[512,128]{0,1:T(8,128)(2,1)S(1)} %copy.134, bf16[512,128]{0,1:T(8,128)(2,1)S(1)} %bitcast.246), kind=kOutput, calls=%fused_computation.3.clone.1.clone | convolution fusion | flops 3640328192 | bytes 3856384 | tf_op jit(solution)/shard_map/while/body/eval_jaxpr/kbw,wc->bkc/dot_general | solution.py:83
  40.9 2.0 constant_dynamic-update-slice_fusion.6
  42.9 2.3 %fusion.86 = bf16[2,512,128]{2,1,0:T(8,128)(2,1)S(1)} fusion(bf16[2,512,128]{2,1,0:T(8,128)(2,1)S(1)} %get-tuple-element.610, s32[]{:T(128)} %get-tuple-element.609, bf16[512,3456]{0,1:T(8,128)(2,1)S(1)} %bitcast.239, bf16[3456,128]{1,0:T(8,128)(2,1)} %get-tuple-element.626), kind=kOutput, calls=%fused_computation.5.clone.1.clone | convolution fusion | flops 452984832 | bytes 4685828 | tf_op jit(solution)/shard_map/while/body/eval_jaxpr/dot_general | solution.py:87
  48.4 13.4 %fusion.85 = bf16[128,27,512]{2,0,1:T(8,128)(2,1)S(1)} fusion(s32[27,512]{1,0:T(8,128)S(1)} %bitcast_select_fusion.6, bf16[512,128]{0,1:T(8,128)(2,1)S(1)} %copy.134, bf16[512,128]{0,1:T(8,128)(2,1)S(1)} %bitcast.246), kind=kOutput, calls=%fused_computation.3.clone.1.clone | convolution fusion | flops 3640328192 | bytes 3856384 | tf_op jit(solution)/shard_map/while/body/eval_jaxpr/kbw,wc->bkc/dot_general | solution.py:83
  61.7 2.0 constant_dynamic-update-slice_fusion.6
  63.8 2.3 %fusion.86 = bf16[2,512,128]{2,1,0:T(8,128)(2,1)S(1)} fusion(bf16[2,512,128]{2,1,0:T(8,128)(2,1)S(1)} %get-tuple-element.610, s32[]{:T(128)} %get-tuple-element.609, bf16[512,3456]{0,1:T(8,128)(2,1)S(1)} %bitcast.239, bf16[3456,128]{1,0:T(8,128)(2,1)} %get-tuple-element.626), kind=kOutput, calls=%fused_computation.5.clone.1.clone | convolution fusion | flops 452984832 | bytes 4685828 | tf_op jit(solution)/shard_map/while/body/eval_jaxpr/dot_general | solution.py:87
  66.7 20.7 %all_to_all.15 = f32[128,3,128]{2,1,0:T(4,128)S(1)} all-to-all(f32[128,3,128]{2,1,0:T(4,128)S(1)} %broadcast_in_dim.72), channel_id=1, replica_groups=mesh['bx'=16,'by'=8] {'bx','by'}, dimensions={0} | all-to-all | bytes 393216 | tf_op jit(solution)/shard_map/all_to_all | solution.py:35
  88.7 4.7 %all-to-all-start.1 = ((f32[128,2,128]{2,1,0:T(2,128)}), f32[128,2,128]{2,1,0:T(2,128)S(1)}, u32[]{:S(2)}, u32[]{:S(2)}) async-start(f32[128,2,128]{2,1,0:T(2,128)} %broadcast_in_dim.75), calls=%async_computation.1 | async-start | bytes 262144 | tf_op jit(solution)/shard_map/all_to_all | solution.py:35
  93.4 9.8 %all-to-all-done.1 = f32[128,2,128]{2,1,0:T(2,128)S(1)} async-done(((f32[128,2,128]{2,1,0:T(2,128)}), f32[128,2,128]{2,1,0:T(2,128)S(1)}, u32[]{:S(2)}, u32[]{:S(2)}) %all-to-all-start.1) | async-done | bytes 131104 | tf_op jit(solution)/shard_map/all_to_all | solution.py:35
  103.4 1.0 fusion.41
  105.0 51.2 %while.34 = (s32[]{:T(128)}, f32[3456,128]{1,0:T(8,128)}, f32[2,512,128]{2,1,0:T(8,128)}, bf16[2,8,64,128]{3,2,0,1:T(8,128)(2,1)}, bf16[2,512,3456]{1,2,0:T(8,12...) while((s32[]{:T(128)}, f32[3456,128]{1,0:T(8,128)}, ...), condition=%wide.region_12.13_spmd.clone.clone, body=%wide.region_11.12_spmd.clone.sunk.clone | while | flops 4547128320 | bytes 45617012 | solution.py:147
  105.0 1.2 dynamic_slice.99
  107.5 1.6 bitcast_select_fusion.7
  109.1 2.3 %convolution_convert_fusion.3 = bf16[512,3456]{1,0:T(8,128)(2,1)S(1)} fusion(bf16[3456,128]{1,0:T(8,128)(2,1)} %get-tuple-element.659, bf16[2,512,128]{2,1,0:T(8,128)(2,1)} %get-tuple-element.656, s32[]{:T(128)} %get-tuple-element.640), kind=kOutput, calls=%fused_computation.28.clone.1.clone | convolution fusion | flops 454754304 | bytes 4555264 | tf_op jit(solution)/shard_map/while/body/eval_jaxpr/dot_general | solution.py:130
  111.4 3.7 %copy.136 = bf16[512,3456]{0,1:T(8,128)(2,1)} copy(bf16[512,3456]{1,0:T(8,128)(2,1)S(1)} %convolution_convert_fusion.3) | data formatting | bytes 7077888 | tf_op jit(solution)/shard_map/while/body/eval_jaxpr/convert_element_type | solution.py:132
  115.1 10.6 %fusion.92 = f32[1024,128]{1,0:T(8,128)S(1)} fusion(bf16[512,27,128]{0,2,1:T(8,128)(2,1)} %bitcast.240, s32[27,512]{1,0:T(8,128)} %bitcast_select_fusion.7), kind=kOutput, calls=%fused_computation.32.clone.1.clone | convolution fusion | flops 3638034432 | bytes 4118528 | tf_op jit(solution)/shard_map/while/body/eval_jaxpr/kbw,bkc->wc/dot_general | solution.py:135
  125.9 3.4 %convolution_add_fusion.3 = f32[3456,128]{1,0:T(8,128)S(1)} fusion(bf16[2,512,3456]{1,2,0:T(8,128)(2,1)} %get-tuple-element.655, s32[]{:T(128)} %get-tuple-element.640, f32[3456,128]{1,0:T(8,128)S(1)} %copy-done, pred[]{:T(512)S(6)} %compare.27, bf16[2,512,128]{2,1,0:T(8,128)(2,1)S(1)} %copy-done.2), kind=kOutput, calls=%fused_computation.29.clone.1.clone | convolution fusion | flops 453869568 | bytes 7209985 | tf_op jit(solution)/shard_map/while/body/eval_jaxpr/dot_general | solution.py:127
  129.4 1.2 copy-done.1
  130.6 1.2 dynamic_slice.99
  133.1 1.6 bitcast_select_fusion.7
  134.6 2.3 %convolution_convert_fusion.3 = bf16[512,3456]{1,0:T(8,128)(2,1)S(1)} fusion(bf16[3456,128]{1,0:T(8,128)(2,1)} %get-tuple-element.659, bf16[2,512,128]{2,1,0:T(8,128)(2,1)} %get-tuple-element.656, s32[]{:T(128)} %get-tuple-element.640), kind=kOutput, calls=%fused_computation.28.clone.1.clone | convolution fusion | flops 454754304 | bytes 4555264 | tf_op jit(solution)/shard_map/while/body/eval_jaxpr/dot_general | solution.py:130
  137.0 3.7 %copy.136 = bf16[512,3456]{0,1:T(8,128)(2,1)} copy(bf16[512,3456]{1,0:T(8,128)(2,1)S(1)} %convolution_convert_fusion.3) | data formatting | bytes 7077888 | tf_op jit(solution)/shard_map/while/body/eval_jaxpr/convert_element_type | solution.py:132
  140.7 10.7 %fusion.92 = f32[1024,128]{1,0:T(8,128)S(1)} fusion(bf16[512,27,128]{0,2,1:T(8,128)(2,1)} %bitcast.240, s32[27,512]{1,0:T(8,128)} %bitcast_select_fusion.7), kind=kOutput, calls=%fused_computation.32.clone.1.clone | convolution fusion | flops 3638034432 | bytes 4118528 | tf_op jit(solution)/shard_map/while/body/eval_jaxpr/kbw,bkc->wc/dot_general | solution.py:135
  151.5 3.4 %convolution_add_fusion.3 = f32[3456,128]{1,0:T(8,128)S(1)} fusion(bf16[2,512,3456]{1,2,0:T(8,128)(2,1)} %get-tuple-element.655, s32[]{:T(128)} %get-tuple-element.640, f32[3456,128]{1,0:T(8,128)S(1)} %copy-done, pred[]{:T(512)S(6)} %compare.27, bf16[2,512,128]{2,1,0:T(8,128)(2,1)S(1)} %copy-done.2), kind=kOutput, calls=%fused_computation.29.clone.1.clone | convolution fusion | flops 453869568 | bytes 7209985 | tf_op jit(solution)/shard_map/while/body/eval_jaxpr/dot_general | solution.py:127
  155.0 1.2 copy-done.1
  156.2 1.0 fusion.50
  158.1 1.6 convert_element_type.148
  159.7 6.1 %reshape.501 = bf16[27,16,8,8,16]{4,3,2,1,0:T(8,128)(2,1)} reshape(bf16[3456,128]{1,0:T(8,128)(2,1)S(1)} %convert_element_type.148) | data formatting | bytes 1769472 | tf_op jit(solution)/shard_map/reshape | solution.py:150
  165.8 7.4 %copy.125 = bf16[16,8,27,8,16]{4,3,2,1,0:T(8,128)(2,1)} copy(bf16[16,8,27,8,16]{4,1,3,0,2:T(8,128)(2,1)} %bitcast.241) | data formatting | bytes 1769472
  173.2 8.0 %reshape.509 = bf16[128,27,128]{2,1,0:T(8,128)(2,1)S(1)} reshape(bf16[16,8,27,8,16]{4,3,2,1,0:T(8,128)(2,1)} %copy.125) | data formatting | bytes 1769472
  181.2 1.1 pad.4.clone
  182.3 4.3 %all-to-all-start.2 = ((bf16[128,32,128]{2,1,0:T(8,128)(2,1)}), bf16[128,32,128]{2,1,0:T(8,128)(2,1)S(1)}, u32[]{:S(2)}, u32[]{:S(2)}) async-start(bf16[128,32,128]{2,1,0:T(8,128)(2,1)} %pad.4.clone), calls=%async_computation.2 | async-start | bytes 2097152 | tf_op jit(solution)/shard_map/all_to_all | solution.py:155
  186.7 3.4 %collective-permute-start.4 = (bf16[1,3,128,128]{3,2,1,0:T(8,128)(2,1)S(1)}, bf16[1,3,128,128]{3,2,1,0:T(8,128)(2,1)S(1)}, u32[]{:S(2)}, u32[]{:S(2)}) collective-permute-start(bf16[1,3,128,128]{3,2,1,0:T(8,128)(2,1)S(1)} %bitcast.274), channel_id=1, source_target_pairs={{0,8},{8,16},{16,24},{24,32},{32,40},{40,48},{48,56},{56,64},{64,7... | collective-permute-start | bytes 294920 | tf_op jit(solution)/shard_map/ppermute | solution.py:18
  190.1 1.3 collective-permute-start.5
  191.5 9.6 %collective-permute-done.4 = bf16[1,3,128,128]{3,2,1,0:T(8,128)(2,1)S(1)} collective-permute-done((bf16[1,3,128,128]{3,2,1,0:T(8,128)(2,1)S(1)}, bf16[1,3,128,128]{3,2,1,0:T(8,128)(2,1)S(1)}, u32[]{:S(2)}, u32[]{:S(2)}) %collective-permute-start.4) | collective-permute-done | bytes 98336 | tf_op jit(solution)/shard_map/ppermute | solution.py:18
  201.0 2.6 %collective-permute-done.5 = bf16[1,3,128,128]{3,2,1,0:T(8,128)(2,1)S(1)} collective-permute-done((bf16[1,3,128,128]{3,2,1,0:T(8,128)(2,1)S(1)}, bf16[1,3,128,128]{3,2,1,0:T(8,128)(2,1)S(1)}, u32[]{:S(2)}, u32[]{:S(2)}) %collective-permute-start.5) | collective-permute-done | bytes 98336 | tf_op jit(solution)/shard_map/ppermute | solution.py:20
  203.7 3.0 %collective-permute-start.6 = (bf16[5,1,128,128]{3,2,1,0:T(8,128)(2,1)S(1)}, bf16[5,1,128,128]{3,2,1,0:T(8,128)(2,1)S(1)}, u32[]{:S(2)}, u32[]{:S(2)}) collective-permute-start(bf16[5,1,128,128]{3,2,1,0:T(8,128)(2,1)S(1)} %get-tuple-element.423), channel_id=1, source_target_pairs={{0,1},{1,2},{2,3},{3,4},{4,5},{5,6},{6,7},{8,9},{9,10},{10,11},{11... | collective-permute-start | bytes 491528 | tf_op jit(solution)/shard_map/ppermute | solution.py:18
  206.7 1.9 collective-permute-start.7
  209.6 3.8 %collective-permute-done.7 = bf16[5,1,128,128]{3,2,1,0:T(8,128)(2,1)S(1)} collective-permute-done((bf16[5,1,128,128]{3,2,1,0:T(8,128)(2,1)S(1)}, bf16[5,1,128,128]{3,2,1,0:T(8,128)(2,1)S(1)}, u32[]{:S(2)}, u32[]{:S(2)}) %collective-permute-start.7) | collective-permute-done | bytes 163872 | tf_op jit(solution)/shard_map/ppermute | solution.py:20
  213.6 2.2 fusion.34
  (123 shorter events, 11.1 us)
Async XLA Ops:
  0.6 18.8 %copy-start.9 = (s32[1,1,27,1024]{3,1,2,0:T(1,128)S(1)}, s32[1,1,27,1024]{3,1,2,0:T(1,128)}, u32[]{:S(2)}) copy-start(s32[1,1,27,1024]{3,1,2,0:T(1,128)} %param.14) | copy-start | bytes 331780
  0.6 23.7 %copy-start.5 = (bf16[1,1,1024,128]{3,2,1,0:T(8,128)(2,1)S(1)}, bf16[1,1,1024,128]{3,2,1,0:T(8,128)(2,1)}, u32[]{:S(2)}) copy-start(bf16[1,1,1024,128]{3,2,1,0:T(8,128)(2,1)} %param.12) | copy-start | bytes 786436
  2.5 6.5 %collective-permute-start = (bf16[1,3,128,128]{3,2,1,0:T(8,128)(2,1)S(1)}, bf16[1,3,128,128]{3,2,1,0:T(8,128)(2,1)S(1)}, u32[]{:S(2)}, u32[]{:S(2)}) collective-permute-start(bf16[1,3,128,128]{3,2,1,0:T(8,128)(2,1)S(1)} %bitcast.276), channel_id=1, source_target_pairs={{0,8},{8,16},{16,24},{24,32},{32,40},{40,48},{48,56},{56,64},{64,7... | collective-permute-start | bytes 294920 | tf_op jit(solution)/shard_map/ppermute | solution.py:18
  6.9 5.5 %collective-permute-start.1 = (bf16[1,3,128,128]{3,2,1,0:T(8,128)(2,1)S(1)}, bf16[1,3,128,128]{3,2,1,0:T(8,128)(2,1)S(1)}, u32[]{:S(2)}, u32[]{:S(2)}) collective-permute-start(bf16[1,3,128,128]{3,2,1,0:T(8,128)(2,1)S(1)} %bitcast.275), channel_id=1, source_target_pairs={{8,0},{16,8},{24,16},{32,24},{40,32},{48,40},{56,48},{64,56},{72,6... | collective-permute-start | bytes 294920 | tf_op jit(solution)/shard_map/ppermute | solution.py:20
  8.3 12.2 %copy-start.13 = (bf16[9]{0:T(256)(128)(2,1)}, bf16[9]{0:T(256)(128)(2,1)S(1)}, u32[]{:S(2)}) copy-start(bf16[9]{0:T(256)(128)(2,1)S(1)} %pad.36.clone) | copy-start | bytes 58
  12.5 8.1 %collective-permute-start.2 = (bf16[5,1,128,128]{3,2,1,0:T(8,128)(2,1)S(1)}, bf16[5,1,128,128]{3,2,1,0:T(8,128)(2,1)S(1)}, u32[]{:S(2)}, u32[]{:S(2)}) collective-permute-start(bf16[5,1,128,128]{3,2,1,0:T(8,128)(2,1)S(1)} %get-tuple-element.425), channel_id=1, source_target_pairs={{0,1},{1,2},{2,3},{3,4},{4,5},{5,6},{6,7},{8,9},{9,10},{10,11},{11... | collective-permute-start | bytes 491528 | tf_op jit(solution)/shard_map/ppermute | solution.py:18
  17.5 6.6 %collective-permute-start.3 = (bf16[5,1,128,128]{3,2,1,0:T(8,128)(2,1)S(1)}, bf16[5,1,128,128]{3,2,1,0:T(8,128)(2,1)S(1)}, u32[]{:S(2)}, u32[]{:S(2)}) collective-permute-start(bf16[5,1,128,128]{3,2,1,0:T(8,128)(2,1)S(1)} %get-tuple-element.426), channel_id=1, source_target_pairs={{1,0},{2,1},{3,2},{4,3},{5,4},{6,5},{7,6},{9,8},{10,9},{11,10},{12... | collective-permute-start | bytes 491528 | tf_op jit(solution)/shard_map/ppermute | solution.py:20
  24.4 63.3 %copy-start.10 = (f32[128]{0:T(128)S(1)}, f32[128]{0:T(128)}, u32[]{:S(2)}) copy-start(f32[128]{0:T(128)} %param.17) | copy-start | bytes 1540
  24.4 63.3 %copy-start.6 = (bf16[1,1,1024,128]{3,2,1,0:T(8,128)(2,1)S(1)}, bf16[1,1,1024,128]{3,2,1,0:T(8,128)(2,1)}, u32[]{:S(2)}) copy-start(bf16[1,1,1024,128]{3,2,1,0:T(8,128)(2,1)} %param.19) | copy-start | bytes 786436
  24.4 63.3 %copy-start.11 = (f32[128]{0:T(128)S(1)}, f32[128]{0:T(128)}, u32[]{:S(2)}) copy-start(f32[128]{0:T(128)} %param.18) | copy-start | bytes 1540
  66.1 38.9 %copy-start.3 = (bf16[2,512,128]{2,1,0:T(8,128)(2,1)}, bf16[2,512,128]{2,1,0:T(8,128)(2,1)S(1)}, u32[]{:S(2)}) copy-start(bf16[2,512,128]{2,1,0:T(8,128)(2,1)S(1)} %get-tuple-element.224) | copy-start | bytes 786436
  88.7 14.6 %all-to-all-start.1 = ((f32[128,2,128]{2,1,0:T(2,128)}), f32[128,2,128]{2,1,0:T(2,128)S(1)}, u32[]{:S(2)}, u32[]{:S(2)}) async-start(f32[128,2,128]{2,1,0:T(2,128)} %broadcast_in_dim.75), calls=%async_computation.1 | async-start | bytes 262144 | tf_op jit(solution)/shard_map/all_to_all | solution.py:35
  115.1 10.7 %copy-start.15 = (f32[2,512,128]{2,1,0:T(8,128)S(1)}, f32[2,512,128]{2,1,0:T(8,128)}, u32[]{:S(2)}) copy-start(f32[2,512,128]{2,1,0:T(8,128)} %get-tuple-element.642) | copy-start | bytes 1572868 | tf_op jit(solution)/shard_map/while
  115.1 10.7 %copy-start.7 = (bf16[2,8,64,128]{3,2,0,1:T(8,128)(2,1)S(1)}, bf16[2,8,64,128]{3,2,0,1:T(8,128)(2,1)}, u32[]{:S(2)}) copy-start(bf16[2,8,64,128]{3,2,0,1:T(8,128)(2,1)} %get-tuple-element.643) | copy-start | bytes 786436 | tf_op jit(solution)/shard_map/while
  115.1 10.8 %copy-start = (f32[3456,128]{1,0:T(8,128)S(1)}, f32[3456,128]{1,0:T(8,128)}, u32[]{:S(2)}) copy-start(f32[3456,128]{1,0:T(8,128)} %get-tuple-element.641) | copy-start | bytes 5308420 | tf_op jit(solution)/shard_map/while
  115.1 10.8 %copy-start.2 = (bf16[2,512,128]{2,1,0:T(8,128)(2,1)S(1)}, bf16[2,512,128]{2,1,0:T(8,128)(2,1)}, u32[]{:S(2)}) copy-start(bf16[2,512,128]{2,1,0:T(8,128)(2,1)} %get-tuple-element.656) | copy-start | bytes 786436 | tf_op jit(solution)/shard_map/while
  125.8 3.5 %copy-start.16 = (f32[2,512,128]{2,1,0:T(8,128)}, f32[2,512,128]{2,1,0:T(8,128)S(1)}, u32[]{:S(2)}) copy-start(f32[2,512,128]{2,1,0:T(8,128)S(1)} %fusion.93) | copy-start | bytes 1572868 | tf_op jit(solution)/shard_map/while
  125.9 3.5 %copy-start.8 = (bf16[2,8,64,128]{3,2,0,1:T(8,128)(2,1)}, bf16[2,8,64,128]{3,2,0,1:T(8,128)(2,1)S(1)}, u32[]{:S(2)}) copy-start(bf16[2,8,64,128]{3,2,0,1:T(8,128)(2,1)S(1)} %constant_dynamic-update-slice_fusion.7) | copy-start | bytes 786436 | tf_op jit(solution)/shard_map/while
  129.4 1.2 copy-start.1
  140.7 10.7 %copy-start.15 = (f32[2,512,128]{2,1,0:T(8,128)S(1)}, f32[2,512,128]{2,1,0:T(8,128)}, u32[]{:S(2)}) copy-start(f32[2,512,128]{2,1,0:T(8,128)} %get-tuple-element.642) | copy-start | bytes 1572868 | tf_op jit(solution)/shard_map/while
  140.7 10.7 %copy-start.7 = (bf16[2,8,64,128]{3,2,0,1:T(8,128)(2,1)S(1)}, bf16[2,8,64,128]{3,2,0,1:T(8,128)(2,1)}, u32[]{:S(2)}) copy-start(bf16[2,8,64,128]{3,2,0,1:T(8,128)(2,1)} %get-tuple-element.643) | copy-start | bytes 786436 | tf_op jit(solution)/shard_map/while
  140.7 10.8 %copy-start = (f32[3456,128]{1,0:T(8,128)S(1)}, f32[3456,128]{1,0:T(8,128)}, u32[]{:S(2)}) copy-start(f32[3456,128]{1,0:T(8,128)} %get-tuple-element.641) | copy-start | bytes 5308420 | tf_op jit(solution)/shard_map/while
  140.7 10.8 %copy-start.2 = (bf16[2,512,128]{2,1,0:T(8,128)(2,1)S(1)}, bf16[2,512,128]{2,1,0:T(8,128)(2,1)}, u32[]{:S(2)}) copy-start(bf16[2,512,128]{2,1,0:T(8,128)(2,1)} %get-tuple-element.656) | copy-start | bytes 786436 | tf_op jit(solution)/shard_map/while
  151.4 3.5 %copy-start.16 = (f32[2,512,128]{2,1,0:T(8,128)}, f32[2,512,128]{2,1,0:T(8,128)S(1)}, u32[]{:S(2)}) copy-start(f32[2,512,128]{2,1,0:T(8,128)S(1)} %fusion.93) | copy-start | bytes 1572868 | tf_op jit(solution)/shard_map/while
  151.5 3.5 %copy-start.8 = (bf16[2,8,64,128]{3,2,0,1:T(8,128)(2,1)}, bf16[2,8,64,128]{3,2,0,1:T(8,128)(2,1)S(1)}, u32[]{:S(2)}) copy-start(bf16[2,8,64,128]{3,2,0,1:T(8,128)(2,1)S(1)} %constant_dynamic-update-slice_fusion.7) | copy-start | bytes 786436 | tf_op jit(solution)/shard_map/while
  155.0 1.2 copy-start.1
  173.2 18.2 %copy-start.14 = (bf16[9]{0:T(256)(128)(2,1)S(1)}, bf16[9]{0:T(256)(128)(2,1)}, u32[]{:S(2)}) copy-start(bf16[9]{0:T(256)(128)(2,1)} %copy-done.13) | copy-start | bytes 58
  181.2 27.4 %copy-start.4 = (bf16[2,512,128]{2,1,0:T(8,128)(2,1)S(1)}, bf16[2,512,128]{2,1,0:T(8,128)(2,1)}, u32[]{:S(2)}) copy-start(bf16[2,512,128]{2,1,0:T(8,128)(2,1)} %copy-done.3) | copy-start | bytes 786436
  181.2 27.4 %copy-start.12 = (f32[128]{0:T(128)S(1)}, f32[128]{0:T(128)}, u32[]{:S(2)}) copy-start(f32[128]{0:T(128)} %param.18) | copy-start | bytes 1540
  181.2 32.3 %copy-start.17 = (f32[2,512,128]{2,1,0:T(8,128)S(1)}, f32[2,512,128]{2,1,0:T(8,128)}, u32[]{:S(2)}) copy-start(f32[2,512,128]{2,1,0:T(8,128)} %get-tuple-element.226) | copy-start | bytes 1572868
  181.2 32.3 %copy-start.18 = (s32[1,1,8,128]{3,2,1,0:T(8,128)S(1)}, s32[1,1,8,128]{3,2,1,0:T(8,128)}, u32[]{:S(2)}) copy-start(s32[1,1,8,128]{3,2,1,0:T(8,128)} %param.15) | copy-start | bytes 12292
  182.3 33.4 %all-to-all-start.2 = ((bf16[128,32,128]{2,1,0:T(8,128)(2,1)}), bf16[128,32,128]{2,1,0:T(8,128)(2,1)S(1)}, u32[]{:S(2)}, u32[]{:S(2)}) async-start(bf16[128,32,128]{2,1,0:T(8,128)(2,1)} %pad.4.clone), calls=%async_computation.2 | async-start | bytes 2097152 | tf_op jit(solution)/shard_map/all_to_all | solution.py:155
  186.7 14.4 %collective-permute-start.4 = (bf16[1,3,128,128]{3,2,1,0:T(8,128)(2,1)S(1)}, bf16[1,3,128,128]{3,2,1,0:T(8,128)(2,1)S(1)}, u32[]{:S(2)}, u32[]{:S(2)}) collective-permute-start(bf16[1,3,128,128]{3,2,1,0:T(8,128)(2,1)S(1)} %bitcast.274), channel_id=1, source_target_pairs={{0,8},{8,16},{16,24},{24,32},{32,40},{40,48},{48,56},{56,64},{64,7... | collective-permute-start | bytes 294920 | tf_op jit(solution)/shard_map/ppermute | solution.py:18
  190.1 13.6 %collective-permute-start.5 = (bf16[1,3,128,128]{3,2,1,0:T(8,128)(2,1)S(1)}, bf16[1,3,128,128]{3,2,1,0:T(8,128)(2,1)S(1)}, u32[]{:S(2)}, u32[]{:S(2)}) collective-permute-start(bf16[1,3,128,128]{3,2,1,0:T(8,128)(2,1)S(1)} %bitcast.273), channel_id=1, source_target_pairs={{8,0},{16,8},{24,16},{32,24},{40,32},{48,40},{56,48},{64,56},{72,6... | collective-permute-start | bytes 294920 | tf_op jit(solution)/shard_map/ppermute | solution.py:20
  203.7 5.9 %collective-permute-start.6 = (bf16[5,1,128,128]{3,2,1,0:T(8,128)(2,1)S(1)}, bf16[5,1,128,128]{3,2,1,0:T(8,128)(2,1)S(1)}, u32[]{:S(2)}, u32[]{:S(2)}) collective-permute-start(bf16[5,1,128,128]{3,2,1,0:T(8,128)(2,1)S(1)} %get-tuple-element.423), channel_id=1, source_target_pairs={{0,1},{1,2},{2,3},{3,4},{4,5},{5,6},{6,7},{8,9},{9,10},{10,11},{11... | collective-permute-start | bytes 491528 | tf_op jit(solution)/shard_map/ppermute | solution.py:18
  206.7 6.6 %collective-permute-start.7 = (bf16[5,1,128,128]{3,2,1,0:T(8,128)(2,1)S(1)}, bf16[5,1,128,128]{3,2,1,0:T(8,128)(2,1)S(1)}, u32[]{:S(2)}, u32[]{:S(2)}) collective-permute-start(bf16[5,1,128,128]{3,2,1,0:T(8,128)(2,1)S(1)} %get-tuple-element.424), channel_id=1, source_target_pairs={{1,0},{2,1},{3,2},{4,3},{5,4},{6,5},{7,6},{9,8},{10,9},{11,10},{12... | collective-permute-start | bytes 491528 | tf_op jit(solution)/shard_map/ppermute | solution.py:20
